TPU v7x, 32 devices: a whole 2x2x4 slice. The times are simulated.
32 devices in a mesh: gx: 4 (over y, x), gy: 8 (over z, core).
Axes of the slice: x: 2, y: 2, z: 4, core: 2. Of those that a mesh axis runs over, the one named last changes fastest.
Arguments:
- cam_pose: float32 [7, 8192], P(None, ('gx', 'gy')), may hold values from -0.5 to 2, as said below
- points: float32 [3, 131072], P(None, ('gx', 'gy')), may hold values from -1.5 to 8, as said below
- obs_uv: float32 [2, 32, 32, 128], P(None, ('gx', 'gy')), may hold values from -0.6 to 0.6
- obs_cam: int32 [32, 32, 128], P(('gx', 'gy')), may hold values from 0 to 255
- obs_pt: int32 [32, 32, 128], P(('gx', 'gy')), may hold values from 0 to 4095
- block_count: int32 [32, 32], P(('gx', 'gy')), may hold values from 1 to 128, as said below
- send_list: int32 [32, 32, 16], P(('gx', 'gy')), may hold values from 0 to 255
- edge_slot: int32 [8, 8192], P(None, ('gx', 'gy')), may hold values from 0 to 511
- edge_weight: float32 [8, 8192], P(None, ('gx', 'gy')), may hold values from 0.2 to 1
Outputs:
- cam_step: float32 [6, 8192], P(None, ('gx', 'gy'))
- cam_residual: float32 [6, 8192], P(None, ('gx', 'gy'))
Inputs may be any that keep to these rules, and one draw needn't show every extreme that they name: `cam_pose`: rows 0 in [0.9, 1.1], rows 1 to 3 in [-0.15, 0.15], rows 4 and 5 in [-0.5, 0.5], row 6 in [1, 2]. `points`: rows 0 and 1 in [-1.5, 1.5], row 2 in [4, 8]. Slot j of block [d, s] is live exactly when j < block_count[d, s]; some blocks are full.
All inputs are finite; a program needn't handle non-finite values.
Results may differ from a plain program's by a relative error of at most 0.00021.
Values sent between devices are 32-bit elements; how exact they have to be, the bound alone decides.
A program may use at most 64 MiB of HBM per device.

v0:
```python
import functools
import math

import jax
import jax.numpy as jnp
from jax import lax
from jax.experimental import pallas as pl
from jax.experimental.pallas import tpu as pltpu
from jax.sharding import PartitionSpec as P

ITERS = 2
DAMPING = 1.0
LANES = 128
MESH = pl.DeviceIdType.MESH
PAIRS = [(a, b) for a in range(6) for b in range(a, 6)]
F32 = jnp.float32
BF16 = jnp.bfloat16


def iota(shape, axis):
    return lax.broadcasted_iota(jnp.int32, shape, axis)


def head(x):
    return x.astype(BF16).astype(F32)


def split2(x):
    high = head(x)
    return jnp.concatenate([high, x - high], 0).astype(BF16)


def split3(x):
    high = head(x)
    rest = x - high
    middle = head(rest)
    return jnp.concatenate([high, middle, rest - middle], 0).astype(BF16)


def dot(a, b):
    return jnp.dot(a, b, preferred_element_type=F32)


def dot_nt(a, b):
    return lax.dot_general(a, b, (((1,), (1,)), ((), ())), preferred_element_type=F32)


def block_transpose(x):
    off = jnp.bitwise_and((iota((8, LANES), 1) >> 4) - iota((8, LANES), 0), 7)
    out = x
    for s in range(1, 8):
        moved = pltpu.roll(pltpu.roll(x, 8 - s, 0), 16 * s, 1)
        out = jnp.where(off == s, moved, out)
    return out


def to_rows(x):
    tiles = x.shape[1] // LANES
    return jnp.concatenate(
        [block_transpose(x[:, t * LANES : (t + 1) * LANES]) for t in range(tiles)], 0
    )


def to_columns(x):
    tiles = x.shape[0] // 8
    return jnp.concatenate([block_transpose(x[8 * t : 8 * t + 8]) for t in range(tiles)], 1)


def kernel(
    nx,
    ny,
    cam_ref,
    pts_ref,
    uv_ref,
    oc_ref,
    op_ref,
    cnt_ref,
    snd_ref,
    es_ref,
    ew_ref,
    step_ref,
    res_ref,
    tx1,
    rx1,
    tx2,
    rx2,
    txc,
    rxc,
    ohp,
    ohc,
    xbuf,
    vbuf,
    acc0,
    acc1,
    tab0,
    tab1,
    gbuf,
    cbuf,
    cacc,
    s_hi,
    s_lo,
    send_sem,
    recv_sem,
):
    devices = nx * ny
    cams = cam_ref.shape[1]
    width = math.gcd(pts_ref.shape[1], 2 * LANES)
    levels = pts_ref.shape[1] // width
    group = math.gcd(devices, 4)
    span = group * LANES
    me = lax.axis_index("gx") * ny + lax.axis_index("gy")

    barrier = pltpu.get_barrier_semaphore()

    def greet(i, c):
        peer = lax.rem(me + i, devices)
        pl.semaphore_signal(
            barrier, inc=1, device_id=(peer // ny, lax.rem(peer, ny)), device_id_type=MESH
        )
        return c

    lax.fori_loop(1, devices, greet, 0)

    def send(rnd, tx, rx, rows):
        def one(i, c):
            peer = lax.rem(me + i, devices)
            pltpu.make_async_remote_copy(
                src_ref=tx.at[pl.ds(peer * rows, rows)],
                dst_ref=rx.at[pl.ds(me * rows, rows)],
                send_sem=send_sem.at[rnd],
                recv_sem=recv_sem.at[rnd],
                device_id=(peer // ny, lax.rem(peer, ny)),
                device_id_type=MESH,
            ).start()
            return c

        lax.fori_loop(1, devices, one, 0)
        rx[pl.ds(me * rows, rows)] = tx[pl.ds(me * rows, rows)]

    def wait(rnd, ref, rows, sem):
        part = ref.at[pl.ds(0, (devices - 1) * rows)]
        pltpu.make_async_copy(part, part, sem.at[rnd]).wait()

    pose = cam_ref[...]
    table = split3(
        jnp.concatenate([jnp.zeros((2, cams), F32), pose[1:4] / pose[0:1], pose[4:7]], 0)
    )
    row8 = iota((8, LANES), 0)

    def gather_poses(i, c):
        rows = [oc_ref[0, pl.ds(i * group + g, 1), :] for g in range(group)]
        onehot = (iota((cams, span), 0) == jnp.concatenate(rows, 1)).astype(F32).astype(BF16)
        ohc[:, pl.ds(pl.multiple_of(i * span, span), span)] = onehot
        got = dot(table, onehot)
        got = got[0:8] + got[8:16] + got[16:24]
        for g in range(group):
            d = i * group + g
            block = got[:, g * LANES : (g + 1) * LANES]
            block = jnp.where(row8 == 0, uv_ref[0, 0, pl.ds(d, 1), :], block)
            block = jnp.where(row8 == 1, uv_ref[1, 0, pl.ds(d, 1), :], block)
            tx1[pl.ds(pl.multiple_of(d * 8, 8), 8), :] = block
        return c

    lax.fori_loop(0, devices // group, gather_poses, 0)
    pl.semaphore_wait(barrier, devices - 1)
    send(0, tx1, rx1, 8)

    def level_mask(i):
        rows = [op_ref[0, pl.ds(i * group + g, 1), :] for g in range(group)]
        row = jnp.concatenate(rows, 1)
        level = row // width
        return row - level * width, (iota((levels, span), 0) == level).astype(F32)

    positions = jnp.concatenate([pts_ref[...], jnp.zeros((5, levels * width), F32)], 0)
    positions = split3(
        jnp.concatenate([positions[:, k * width : (k + 1) * width] for k in range(levels)], 0)
    )
    part = levels * 8

    def gather_tracks(i, c):
        low, mask = level_mask(i)
        onehot = (iota((width, span), 0) == low).astype(F32).astype(BF16)
        ohp[:, pl.ds(pl.multiple_of(i * span, span), span)] = onehot
        got = dot(positions, onehot)
        got = got[0:part] + got[part : 2 * part] + got[2 * part : 3 * part]
        total = jnp.zeros((8, span), F32)
        for k in range(levels):
            total = total + got[k * 8 : k * 8 + 8] * mask[k : k + 1]
        for g in range(group):
            d = i * group + g
            xbuf[pl.ds(pl.multiple_of(d * 8, 8), 8), :] = total[:, g * LANES : (g + 1) * LANES]
        return c

    lax.fori_loop(0, devices // group, gather_tracks, 0)

    slots = snd_ref.shape[1]
    piece = 64

    def weigh(i, c):
        slot = iota((piece, cams), 0) + i * piece
        total = jnp.zeros((piece, cams), F32)
        for k in range(es_ref.shape[0]):
            total = total + jnp.where(slot == es_ref[k : k + 1, :], ew_ref[k : k + 1, :], 0.0)
        high = head(total)
        at = pl.ds(pl.multiple_of(i * piece, piece), piece)
        s_hi[at, :] = high.astype(BF16)
        s_lo[at, :] = (total - high).astype(BF16)
        return c

    lax.fori_loop(0, slots // piece, weigh, 0)
    ohs = (iota((cams, slots), 0) == snd_ref[...]).astype(F32).astype(BF16)
    degree = jnp.sum(ew_ref[...], 0, keepdims=True)
    ones = jnp.ones((16, cams), F32).astype(BF16)
    slot_degree = (dot_nt(ones, s_hi[...]) + dot_nt(ones, s_lo[...]))[0:1]

    spread = jnp.where(
        iota((devices, devices), 0) == iota((devices, devices), 1), cnt_ref[...].astype(F32), 0.0
    )
    count = jnp.sum(spread, 1, keepdims=True)
    live = (iota((devices, LANES), 1).astype(F32) < count).astype(F32)

    vbuf[...] = jnp.zeros_like(vbuf)
    acc0[...] = jnp.zeros_like(acc0)
    acc1[...] = jnp.zeros_like(acc1)
    tab0[...] = jnp.zeros_like(tab0)
    tab1[...] = jnp.zeros_like(tab1)
    cbuf[...] = jnp.zeros_like(cbuf)
    cacc[...] = jnp.zeros_like(cacc)

    wait(0, rx1, 8, recv_sem)

    def pick(ref, r, stride):
        return ref[pl.ds(r, devices, stride=stride), :]

    mu, mv, q1, q2, q3, t0, t1, t2 = [pick(rx1, r, 8) for r in range(8)]
    x0, x1, x2 = [pick(xbuf, r, 8) for r in range(3)]
    norm = 1.0 / (1.0 + q1 * q1 + q2 * q2 + q3 * q3)
    rot = [
        1.0 + q1 * q1 - q2 * q2 - q3 * q3,
        2.0 * (q1 * q2 - q3),
        2.0 * (q1 * q3 + q2),
        2.0 * (q1 * q2 + q3),
        1.0 - q1 * q1 + q2 * q2 - q3 * q3,
        2.0 * (q2 * q3 - q1),
        2.0 * (q1 * q3 - q2),
        2.0 * (q2 * q3 + q1),
        1.0 - q1 * q1 - q2 * q2 + q3 * q3,
    ]
    rot = [r * norm for r in rot]
    pa = rot[0] * x0 + rot[1] * x1 + rot[2] * x2 + t0
    pb = rot[3] * x0 + rot[4] * x1 + rot[5] * x2 + t1
    pe = rot[6] * x0 + rot[7] * x1 + rot[8] * x2 + t2
    inv = 1.0 / pe
    u = pa * inv
    v = pb * inv
    scaled = inv * live
    ru = (u - mu) * live
    rv = (v - mv) * live
    ju = [scaled * (rot[k] - u * rot[6 + k]) for k in range(3)]
    jv = [scaled * (rot[3 + k] - v * rot[6 + k]) for k in range(3)]
    terms = [ju[k] * ju[l] + jv[k] * jv[l] for k in range(3) for l in range(k, 3)]
    terms = terms + [ju[k] * ru + jv[k] * rv for k in range(3)]
    for r in range(8):
        vbuf[pl.ds(r, devices, stride=16), :] = terms[r]
    vbuf[pl.ds(8, devices, stride=16), :] = head(terms[8])
    vbuf[pl.ds(9, devices, stride=16), :] = terms[8] - head(terms[8])

    def scatter_tracks(i, c):
        _, mask = level_mask(i)
        blocks = [
            vbuf[pl.ds(pl.multiple_of((i * group + g) * 16, 16), 16), :] for g in range(group)
        ]
        block = jnp.concatenate(blocks, 1)
        high = head(block[0:8])
        rows = jnp.concatenate([high, block[0:8] - high, block[8:16]], 0)
        left = jnp.concatenate([rows * mask[k : k + 1] for k in range(levels)], 0).astype(BF16)
        added = dot_nt(left, ohp[:, pl.ds(pl.multiple_of(i * span, span), span)])
        acc0[...] += added[:, 0:LANES]
        acc1[...] += added[:, LANES:]
        return c

    lax.fori_loop(0, devices // group, scatter_tracks, 0)

    for acc, tab in ((acc0, tab0), (acc1, tab1)):

        def take(r):
            return acc[pl.ds(r, levels, stride=24), :]

        def put(r, value):
            tab[pl.ds(r, levels, stride=24), :] = value

        sums = [take(r) + take(8 + r) for r in range(8)] + [take(16) + take(17)]
        h0, h1, h2, h3, h4, h5 = sums[0:6]
        h0, h3, h5 = h0 + DAMPING, h3 + DAMPING, h5 + DAMPING
        cof = [
            h3 * h5 - h4 * h4,
            h2 * h4 - h1 * h5,
            h1 * h4 - h2 * h3,
            h0 * h5 - h2 * h2,
            h1 * h2 - h0 * h4,
            h0 * h3 - h1 * h1,
        ]
        invdet = 1.0 / (h0 * cof[0] + h1 * cof[1] + h2 * cof[2])
        cof = [value * invdet for value in cof]
        g0, g1, g2 = sums[6:9]
        cof = cof + [
            cof[0] * g0 + cof[1] * g1 + cof[2] * g2,
            cof[1] * g0 + cof[3] * g1 + cof[4] * g2,
            cof[2] * g0 + cof[4] * g1 + cof[5] * g2,
        ]
        for r in range(8):
            put(r, head(cof[r]))
            put(8 + r, cof[r] - head(cof[r]))
        put(16, head(cof[8]))
        put(17, cof[8] - head(cof[8]))

    inverse = jnp.concatenate([tab0[...], tab1[...]], 1).astype(BF16)

    def gather_inverse(i, c):
        _, mask = level_mask(i)
        got = dot(inverse, ohp[:, pl.ds(pl.multiple_of(i * span, span), span)])
        total = jnp.zeros((24, span), F32)
        for k in range(levels):
            total = total + got[k * 24 : k * 24 + 24] * mask[k : k + 1]
        total = jnp.concatenate([total[0:8] + total[8:16], total[16:24]], 0)
        for g in range(group):
            at = pl.ds(pl.multiple_of((i * group + g) * 16, 16), 16)
            gbuf[at, :] = total[:, g * LANES : (g + 1) * LANES]
        return c

    lax.fori_loop(0, devices // group, gather_inverse, 0)

    n = [pick(gbuf, r, 16) for r in range(8)]
    n.append(pick(gbuf, 8, 16) + pick(gbuf, 9, 16))
    full = [[n[0], n[1], n[2]], [n[1], n[3], n[4]], [n[2], n[4], n[5]]]
    nu = [sum(full[k][l] * ju[l] for l in range(3)) for k in range(3)]
    nv = [sum(full[k][l] * jv[l] for l in range(3)) for k in range(3)]
    out = [
        live - sum(ju[k] * nu[k] for k in range(3)),
        -sum(ju[k] * nv[k] for k in range(3)),
        live - sum(jv[k] * nv[k] for k in range(3)),
        ru - sum(ju[k] * n[6 + k] for k in range(3)),
        rv - sum(jv[k] * n[6 + k] for k in range(3)),
        inv,
        u,
        v,
    ]
    for r in range(8):
        tx2[pl.ds(r, devices, stride=8), :] = out[r]
    send(1, tx2, rx2, 8)
    wait(1, rx2, 8, recv_sem)

    muu, muv, mvv, eu, ev, inv, u, v = [pick(rx2, r, 8) for r in range(8)]
    cu = [-u * v, 1.0 + u * u, -v, inv, None, -u * inv]
    cv = [-1.0 - v * v, u * v, u, None, inv, -v * inv]

    def combine(first, second):
        kept = [a * b for a, b in (first, second) if b is not None]
        return kept[0] if len(kept) == 1 else kept[0] + kept[1]

    wu = [combine((muu, cu[a]), (muv, cv[a])) for a in range(6)]
    wv = [combine((muv, cu[a]), (mvv, cv[a])) for a in range(6)]
    for r, (a, b) in enumerate(PAIRS):
        cbuf[pl.ds(r, devices, stride=32), :] = combine((wu[a], cu[b]), (wv[a], cv[b]))
    for a in range(6):
        cbuf[pl.ds(21 + a, devices, stride=32), :] = combine((eu, cu[a]), (ev, cv[a]))

    def scatter_cameras(i, c):
        blocks = [
            cbuf[pl.ds(pl.multiple_of((i * group + g) * 32, 32), 32), :] for g in range(group)
        ]
        left = split2(jnp.concatenate(blocks, 1))
        cacc[...] += dot_nt(left, ohc[:, pl.ds(pl.multiple_of(i * span, span), span)])
        return c

    lax.fori_loop(0, devices // group, scatter_cameras, 0)
    sums = cacc[0:32] + cacc[32:64]

    zeros2 = jnp.zeros((2, cams), F32)
    spot = {}
    for r, (a, b) in enumerate(PAIRS):
        spot[a, b] = r
        spot[b, a] = r
    columns = [
        jnp.concatenate([sums[spot[a, b] : spot[a, b] + 1] for a in range(6)] + [zeros2], 0)
        for b in range(6)
    ]
    diagonal = DAMPING + jnp.concatenate(
        [sums[spot[a, a] : spot[a, a] + 1] for a in range(6)] + [zeros2], 0
    )
    keep = iota((8, slots), 0) < 6
    flag = jnp.logical_and(
        iota((8, slots), 0) == 6, jnp.bitwise_and(iota((8, slots), 1), 15) == 0
    )

    def total_of(x):
        return jnp.sum(jnp.sum(x, 0, keepdims=True), 1, keepdims=True)

    def exchange(rnd, values, scalar):
        txc[rnd] = to_rows(jnp.where(flag, scalar, values))
        send(2 + rnd, txc.at[rnd], rxc.at[rnd], 1)
        wait(2 + rnd, rxc.at[rnd], 1, recv_sem)
        raw = to_columns(rxc[rnd])
        return jnp.where(keep, raw, 0.0), total_of(jnp.where(flag, raw, 0.0))

    def to_slots(x):
        got = dot(split3(x), ohs)
        return got[0:8] + got[8:16] + got[16:24]

    def from_slots(x):
        got = dot_nt(split3(x), ohs)
        return got[0:8] + got[8:16] + got[16:24]

    def near(x):
        x = split2(x)
        got = dot(x, s_hi[...]) + dot(x, s_lo[...])
        return got[0:8] + got[8:16]

    def flow(x):
        x = split2(x)
        got = dot_nt(x, s_hi[...]) + dot_nt(x, s_lo[...])
        return got[0:8] + got[8:16]

    residual = -jnp.concatenate([sums[21:27], zeros2], 0)
    step = jnp.zeros((8, cams), F32)
    precond = residual / diagonal
    direction = incoming = rz = None
    for it in range(ITERS):
        arrived, new = exchange(2 * it, to_slots(precond), total_of(residual * precond))
        if it == 0:
            direction, incoming = precond, arrived
        else:
            beta = new / rz
            direction = precond + beta * direction
            incoming = arrived + beta * incoming
        rz = new
        around = near(incoming)
        local = (DAMPING + degree) * direction - around
        for b in range(6):
            local = local + columns[b] * direction[b : b + 1]
        energy = total_of(direction * (local - around)) + total_of(
            slot_degree * incoming * incoming
        )
        back, curve = exchange(2 * it + 1, flow(direction) - slot_degree * incoming, energy)
        image = local - from_slots(back)
        alpha = rz / curve
        step = step + alpha * direction
        residual = residual - alpha * image
        if it + 1 < ITERS:
            precond = residual / diagonal
    step_ref[...] = step[0:6]
    res_ref[...] = residual[0:6]
    wait(0, tx1, 8, send_sem)
    wait(1, tx2, 8, send_sem)
    for rnd in range(2 * ITERS):
        wait(2 + rnd, txc.at[rnd], 1, send_sem)


def per_device(nx, ny, cam_pose, points, uv, obs_cam, obs_pt, count, send_list, es, ew):
    devices = nx * ny
    cams = cam_pose.shape[1]
    width = math.gcd(points.shape[1], 2 * LANES)
    levels = points.shape[1] // width
    slots = devices * send_list.shape[-1]
    vmem = pltpu.VMEM
    rounds = 2 * ITERS
    return pl.pallas_call(
        functools.partial(kernel, nx, ny),
        out_shape=[jax.ShapeDtypeStruct((6, cams), F32)] * 2,
        in_specs=[pl.BlockSpec(memory_space=vmem)] * 9,
        out_specs=[pl.BlockSpec(memory_space=vmem)] * 2,
        scratch_shapes=[
            vmem((devices * 8, LANES), F32),
            vmem((devices * 8, LANES), F32),
            vmem((devices * 8, LANES), F32),
            vmem((devices * 8, LANES), F32),
            vmem((rounds, devices, LANES), F32),
            vmem((rounds, devices, LANES), F32),
            vmem((width, devices * LANES), BF16),
            vmem((cams, devices * LANES), BF16),
            vmem((devices * 8, LANES), F32),
            vmem((devices * 16, LANES), F32),
            vmem((levels * 24, LANES), F32),
            vmem((levels * 24, LANES), F32),
            vmem((levels * 24, LANES), F32),
            vmem((levels * 24, LANES), F32),
            vmem((devices * 16, LANES), F32),
            vmem((devices * 32, LANES), F32),
            vmem((64, cams), F32),
            vmem((slots, cams), BF16),
            vmem((slots, cams), BF16),
            pltpu.SemaphoreType.DMA((2 + rounds,)),
            pltpu.SemaphoreType.DMA((2 + rounds,)),
        ],
        compiler_params=pltpu.CompilerParams(collective_id=0, has_side_effects=True),
    )(cam_pose, points, uv, obs_cam, obs_pt, count, send_list.reshape(1, slots), es, ew)


def solution(mesh):
    both = ("gx", "gy")
    return jax.shard_map(
        functools.partial(per_device, mesh.shape["gx"], mesh.shape["gy"]),
        mesh=mesh,
        in_specs=(
            P(None, both),
            P(None, both),
            P(None, both, None, None),
            P(both, None, None),
            P(both, None, None),
            P(both, None),
            P(both, None, None),
            P(None, both),
            P(None, both),
        ),
        out_specs=(P(None, both), P(None, both)),
        check_vma=False,
    )
```

profile of v0, /device:TPU:0, one launch (start us, length us, event | category | flops | bytes accessed | tf_op | source)
XLA Modules:
  0.0 50.9 jit_solution(13537466147539125133)
XLA Ops:
  0.6 0.8 %copy.12 = s32[1,32,16]{2,1,0:T(8,128)S(1)} copy(s32[1,32,16]{1,2,0:T(8,128)} %param.15) | data formatting | bytes 4096 | tf_op args[6]
  1.4 0.7 %reshape.7.snd_ref = s32[1,512]{1,0:T(1,128)} reshape(s32[1,32,16]{2,1,0:T(8,128)S(1)} %copy.12) | data formatting | bytes 4096 | tf_op jit(solution)/shard_map/reshape | solution.py:496
  2.1 47.0 %shard_map.104 = (f32[6,256]{1,0:T(8,128)}, f32[6,256]{1,0:T(8,128)}) custom-call(f32[7,256]{1,0:T(8,128)} %cam_ref.1, f32[3,4096]{1,0:T(4,128)} %pts_ref.1, f32[2,1,32,128]{3,2,1,0:T(8,128)} %uv_ref.1, s32[1,32,128]{2,1,0:T(8,128)} %oc_ref.1, s32[1,32,128]{2,1,0:T(8,128)} %op_ref.1, s32[1,32]{1,0:T(1,128)} %cnt_ref.1, s32[1,512]{1,0:T(1,128)} %reshape.7.snd_ref, ...), custom_call_target="tpu_custom_call" | custom-call | tf_op jit(solution)/shard_map/pallas_call | solution.py:467
  49.0 0.0 copy-start
  49.0 1.3 %copy.15 = f32[6,256]{1,0:T(8,128)} copy(f32[6,256]{1,0:T(8,128)} %get-tuple-element.4) | data formatting | bytes 12288
  50.3 0.0 copy-done
  50.3 0.6 %copy.16 = f32[6,256]{1,0:T(8,128)} copy(f32[6,256]{1,0:T(8,128)S(1)} %copy-done) | data formatting | bytes 12288
Async XLA Ops:
  49.0 1.3 %copy-start = (f32[6,256]{1,0:T(8,128)S(1)}, f32[6,256]{1,0:T(8,128)}, u32[]{:S(2)}) copy-start(f32[6,256]{1,0:T(8,128)} %get-tuple-element.5) | copy-start | bytes 18436
where the time goes:
time: 51.2 us; the launch traced here: 50.9 us
  Pallas kernels  47 us (92%)
  local copies, waits for them, and re-layouts  3.34 us (7%)
  between operations  0.65 us (1%)
    pallas_call x1, Pallas kernels, per_device(): pl.pallas_call(functools.partial(kernel, nx, ny), out_shape=[jax.ShapeDty...  47 us
    unnamed x5, local copies, waits for them, and re-layouts  2.68 us

commit v1 on v0

--- a/solution.py
+++ b/solution.py
@@ -69,6 +69,16 @@
 def kernel(
     nx,
     ny,
+    cam_hbm,
+    pts_hbm,
+    uv_hbm,
+    oc_hbm,
+    op_hbm,
+    cnt_hbm,
+    snd_hbm,
+    es_hbm,
+    ew_hbm,
+    out_ref,
     cam_ref,
     pts_ref,
     uv_ref,
@@ -78,8 +88,6 @@
     snd_ref,
     es_ref,
     ew_ref,
-    step_ref,
-    res_ref,
     tx1,
     rx1,
     tx2,
@@ -101,12 +109,15 @@
     s_lo,
     send_sem,
     recv_sem,
+    load_sem,
 ):
+    held_refs = (cam_ref, oc_ref, uv_ref, pts_ref, op_ref, es_ref, ew_ref, snd_ref, cnt_ref)
+    hbm = (cam_hbm, oc_hbm, uv_hbm, pts_hbm, op_hbm, es_hbm, ew_hbm, snd_hbm, cnt_hbm)
     devices = nx * ny
     cams = cam_ref.shape[1]
     width = math.gcd(pts_ref.shape[1], 2 * LANES)
     levels = pts_ref.shape[1] // width
-    group = math.gcd(devices, 4)
+    group = math.gcd(devices, 8)
     span = group * LANES
     me = lax.axis_index("gx") * ny + lax.axis_index("gy")
 
@@ -119,7 +130,15 @@
         )
         return c
 
-    lax.fori_loop(1, devices, greet, 0)
+    lax.fori_loop(1, devices, greet, 0, unroll=min(devices - 1, 31))
+    loads = [
+        pltpu.make_async_copy(far, close, load_sem.at[k])
+        for k, (far, close) in enumerate(zip(hbm, held_refs))
+    ]
+    for load in loads:
+        load.start()
+    for load in loads[0:3]:
+        load.wait()
 
     def send(rnd, tx, rx, rows):
         def one(i, c):
@@ -134,7 +153,7 @@
             ).start()
             return c
 
-        lax.fori_loop(1, devices, one, 0)
+        lax.fori_loop(1, devices, one, 0, unroll=min(devices - 1, 31))
         rx[pl.ds(me * rows, rows)] = tx[pl.ds(me * rows, rows)]
 
     def wait(rnd, ref, rows, sem):
@@ -165,6 +184,9 @@
     pl.semaphore_wait(barrier, devices - 1)
     send(0, tx1, rx1, 8)
 
+    for load in loads[3:]:
+        load.wait()
+
     def level_mask(i):
         rows = [op_ref[0, pl.ds(i * group + g, 1), :] for g in range(group)]
         row = jnp.concatenate(rows, 1)
@@ -193,7 +215,8 @@
 
     lax.fori_loop(0, devices // group, gather_tracks, 0)
 
-    slots = snd_ref.shape[1]
+    each = snd_ref.shape[1]
+    slots = devices * each
     piece = 64
 
     def weigh(i, c):
@@ -208,10 +231,19 @@
         return c
 
     lax.fori_loop(0, slots // piece, weigh, 0)
-    ohs = (iota((cams, slots), 0) == snd_ref[...]).astype(F32).astype(BF16)
+    listed = snd_ref[0].astype(F32)
+    tiled = iota((devices, slots), 1) // each == iota((devices, slots), 0)
+    tiled = tiled.astype(F32).astype(BF16)
+    listed = dot(head(listed).astype(BF16), tiled) + dot(
+        (listed - head(listed)).astype(BF16), tiled
+    )
+    own = lax.rem(iota((each, slots), 1), each) == iota((each, slots), 0)
+    listed = jnp.sum(jnp.where(own, listed, 0.0), 0, keepdims=True)
+    ohs = (iota((cams, slots), 0).astype(F32) == listed).astype(F32).astype(BF16)
     degree = jnp.sum(ew_ref[...], 0, keepdims=True)
     ones = jnp.ones((16, cams), F32).astype(BF16)
-    slot_degree = (dot_nt(ones, s_hi[...]) + dot_nt(ones, s_lo[...]))[0:1]
+    slot_degree = (dot_nt(ones, s_hi[...]) + dot_nt(ones, s_lo[...]))[0:8]
+    row_degree = to_rows(slot_degree)
 
     spread = jnp.where(
         iota((devices, devices), 0) == iota((devices, devices), 1), cnt_ref[...].astype(F32), 0.0
@@ -388,20 +420,19 @@
     diagonal = DAMPING + jnp.concatenate(
         [sums[spot[a, a] : spot[a, a] + 1] for a in range(6)] + [zeros2], 0
     )
-    keep = iota((8, slots), 0) < 6
-    flag = jnp.logical_and(
-        iota((8, slots), 0) == 6, jnp.bitwise_and(iota((8, slots), 1), 15) == 0
-    )
+    lane = iota((devices, LANES), 1)
+    held = 6 * each
 
     def total_of(x):
         return jnp.sum(jnp.sum(x, 0, keepdims=True), 1, keepdims=True)
 
-    def exchange(rnd, values, scalar):
-        txc[rnd] = to_rows(jnp.where(flag, scalar, values))
+    def start(rnd, rows):
+        txc[rnd] = rows
         send(2 + rnd, txc.at[rnd], rxc.at[rnd], 1)
+
+    def finish(rnd):
         wait(2 + rnd, rxc.at[rnd], 1, recv_sem)
-        raw = to_columns(rxc[rnd])
-        return jnp.where(keep, raw, 0.0), total_of(jnp.where(flag, raw, 0.0))
+        return rxc[rnd]
 
     def to_slots(x):
         got = dot(split3(x), ohs)
@@ -421,35 +452,57 @@
         got = dot_nt(x, s_hi[...]) + dot_nt(x, s_lo[...])
         return got[0:8] + got[8:16]
 
+    def block_product(x):
+        total = (DAMPING + degree) * x
+        for b in range(6):
+            total = total + columns[b] * x[b : b + 1]
+        return total
+
     residual = -jnp.concatenate([sums[21:27], zeros2], 0)
+    inverse_diagonal = 1.0 / diagonal
     step = jnp.zeros((8, cams), F32)
-    precond = residual / diagonal
-    direction = incoming = rz = None
+    precond = residual * inverse_diagonal
+    rows = to_rows(to_slots(precond))
+    direction = image = curve = rz = None
     for it in range(ITERS):
-        arrived, new = exchange(2 * it, to_slots(precond), total_of(residual * precond))
+        start(2 * it, rows)
+        local = block_product(precond)
+        flowing = to_rows(flow(precond))
+        energy = total_of(precond * local)
+        new = total_of(residual * precond)
+        mixed = new if it == 0 else total_of(precond * image)
+        arrived = finish(2 * it)
+        weighed = row_degree * arrived
+        energy = energy + total_of(arrived * (weighed - 2.0 * flowing))
+        sent = flowing - weighed
+        sent = jnp.where(lane == held + 1, new, sent)
+        sent = jnp.where(lane == held + 2, mixed, sent)
+        sent = jnp.where(lane == held, energy, sent)
+        start(2 * it + 1, sent)
+        local = local - near(to_columns(arrived))
+        back = finish(2 * it + 1)
+        added = jnp.sum(back, 0, keepdims=True)
+        energy, new, mixed = [
+            jnp.sum(jnp.where(lane[0:1] == held + k, added, 0.0), 1, keepdims=True)
+            for k in range(3)
+        ]
+        fresh = local - from_slots(to_columns(jnp.where(lane < held, back, 0.0)))
         if it == 0:
-            direction, incoming = precond, arrived
+            direction, image, curve = precond, fresh, energy
         else:
             beta = new / rz
             direction = precond + beta * direction
-            incoming = arrived + beta * incoming
+            image = fresh + beta * image
+            curve = energy + beta * (2.0 * mixed + beta * curve)
         rz = new
-        around = near(incoming)
-        local = (DAMPING + degree) * direction - around
-        for b in range(6):
-            local = local + columns[b] * direction[b : b + 1]
-        energy = total_of(direction * (local - around)) + total_of(
-            slot_degree * incoming * incoming
-        )
-        back, curve = exchange(2 * it + 1, flow(direction) - slot_degree * incoming, energy)
-        image = local - from_slots(back)
         alpha = rz / curve
+        if it + 1 < ITERS:
+            rows = rows - alpha * to_rows(to_slots(image * inverse_diagonal))
         step = step + alpha * direction
         residual = residual - alpha * image
-        if it + 1 < ITERS:
-            precond = residual / diagonal
-    step_ref[...] = step[0:6]
-    res_ref[...] = residual[0:6]
+        precond = residual * inverse_diagonal
+    out_ref[0] = step[0:6]
+    out_ref[1] = residual[0:6]
     wait(0, tx1, 8, send_sem)
     wait(1, tx2, 8, send_sem)
     for rnd in range(2 * ITERS):
@@ -462,14 +515,17 @@
     width = math.gcd(points.shape[1], 2 * LANES)
     levels = points.shape[1] // width
     slots = devices * send_list.shape[-1]
+    turned = jnp.swapaxes(send_list, 1, 2)
+    operands = (cam_pose, points, uv, obs_cam, obs_pt, count, turned, es, ew)
     vmem = pltpu.VMEM
     rounds = 2 * ITERS
-    return pl.pallas_call(
+    out = pl.pallas_call(
         functools.partial(kernel, nx, ny),
-        out_shape=[jax.ShapeDtypeStruct((6, cams), F32)] * 2,
-        in_specs=[pl.BlockSpec(memory_space=vmem)] * 9,
-        out_specs=[pl.BlockSpec(memory_space=vmem)] * 2,
-        scratch_shapes=[
+        out_shape=jax.ShapeDtypeStruct((2, 6, cams), F32),
+        in_specs=[pl.BlockSpec(memory_space=pl.ANY)] * 9,
+        out_specs=pl.BlockSpec(memory_space=vmem),
+        scratch_shapes=[vmem(x.shape, x.dtype) for x in operands]
+        + [
             vmem((devices * 8, LANES), F32),
             vmem((devices * 8, LANES), F32),
             vmem((devices * 8, LANES), F32),
@@ -491,9 +547,11 @@
             vmem((slots, cams), BF16),
             pltpu.SemaphoreType.DMA((2 + rounds,)),
             pltpu.SemaphoreType.DMA((2 + rounds,)),
+            pltpu.SemaphoreType.DMA((len(operands),)),
         ],
         compiler_params=pltpu.CompilerParams(collective_id=0, has_side_effects=True),
-    )(cam_pose, points, uv, obs_cam, obs_pt, count, send_list.reshape(1, slots), es, ew)
+    )(*operands)
+    return out[0], out[1]
 
 
 def solution(mesh):

time: 51.2 us -> 44.8 us (0.87)
  Pallas kernels: 47 us -> 42.5 us
  local copies, waits for them, and re-layouts: 3.34 us -> 1.32 us
    pallas_call x1, Pallas kernels: 47 us -> 42.5 us  [per_device(): pl.pallas_call(functools.partial(kernel, nx, ny), out_shape=jax.ShapeDtyp...]
    unnamed x5 -> x0, local copies, waits for them, and re-layouts: 2.68 us -> none
    squeeze x0 -> x1, local copies, waits for them, and re-layouts: none -> 1.32 us  [per_device(): return (out[0], out[1])]
    reshape x1 -> x0, local copies, waits for them, and re-layouts: 0.66 us -> none  [per_device(): send_list.reshape(1, slots)]
where the time goes in v1:
time: 44.8 us; the launch traced here: 44.5 us
  Pallas kernels  42.5 us (95%)
  local copies, waits for them, and re-layouts  1.32 us (3%)
  between operations  0.64 us (1%)
    pallas_call x1, Pallas kernels, per_device(): pl.pallas_call(functools.partial(kernel, nx, ny), out_shape=jax.ShapeDtyp...  42.5 us
    squeeze x1, local copies, waits for them, and re-layouts, per_device(): return (out[0], out[1])  1.32 us

profile of v1, /device:TPU:0, one launch (start us, length us, event | category | flops | bytes accessed | tf_op | source)
XLA Modules:
  0.0 44.5 jit_solution(15234078389387018659)
XLA Ops:
  0.6 42.5 %shard_map.104 = f32[2,6,256]{2,1,0:T(8,128)} custom-call(f32[7,256]{1,0:T(8,128)} %cam_hbm.1, f32[3,4096]{1,0:T(4,128)} %pts_hbm.1, f32[2,1,32,128]{3,2,1,0:T(8,128)} %uv_hbm.1, s32[1,32,128]{2,1,0:T(8,128)} %oc_hbm.1, s32[1,32,128]{2,1,0:T(8,128)} %op_hbm.1, s32[1,32]{1,0:T(1,128)} %cnt_hbm.1, s32[1,16,32]{2,1,0:T(8,128)} %bitcast.5, s32[8,256]{1,0:T(8,128)} %es_hbm.1, ...), custom_call_target="tpu_custom_call" | custom-call | tf_op jit(solution)/shard_map/pallas_call | solution.py:522
  43.2 1.3 %slice_bitcast_fusion = (f32[6,256]{1,0:T(8,128)}, f32[6,256]{1,0:T(8,128)}) fusion(f32[2,6,256]{2,1,0:T(8,128)} %shard_map.104), kind=kLoop, calls=%fused_computation | loop fusion | bytes 24576 | tf_op jit(solution)/shard_map/squeeze | solution.py:554

commit v2 on v1

--- a/solution.py
+++ b/solution.py
@@ -103,6 +103,7 @@
     tab0,
     tab1,
     gbuf,
+    kept,
     cbuf,
     cacc,
     s_hi,
@@ -140,17 +141,19 @@
     for load in loads[0:3]:
         load.wait()
 
+    def send_one(rnd, tx, rx, rows, peer):
+        pltpu.make_async_remote_copy(
+            src_ref=tx.at[pl.ds(peer * rows, rows)],
+            dst_ref=rx.at[pl.ds(me * rows, rows)],
+            send_sem=send_sem.at[rnd],
+            recv_sem=recv_sem.at[rnd],
+            device_id=(peer // ny, lax.rem(peer, ny)),
+            device_id_type=MESH,
+        ).start()
+
     def send(rnd, tx, rx, rows):
         def one(i, c):
-            peer = lax.rem(me + i, devices)
-            pltpu.make_async_remote_copy(
-                src_ref=tx.at[pl.ds(peer * rows, rows)],
-                dst_ref=rx.at[pl.ds(me * rows, rows)],
-                send_sem=send_sem.at[rnd],
-                recv_sem=recv_sem.at[rnd],
-                device_id=(peer // ny, lax.rem(peer, ny)),
-                device_id_type=MESH,
-            ).start()
+            send_one(rnd, tx, rx, rows, lax.rem(me + i, devices))
             return c
 
         lax.fori_loop(1, devices, one, 0, unroll=min(devices - 1, 31))
@@ -348,7 +351,11 @@
 
     inverse = jnp.concatenate([tab0[...], tab1[...]], 1).astype(BF16)
 
-    def gather_inverse(i, c):
+    for r, value in enumerate(ju + jv + [ru, rv, inv, u, v, live]):
+        kept[r] = value
+
+    def give_back(step_index, c):
+        i = lax.rem(me // group + 1 + step_index, devices // group)
         _, mask = level_mask(i)
         got = dot(inverse, ohp[:, pl.ds(pl.multiple_of(i * span, span), span)])
         total = jnp.zeros((24, span), F32)
@@ -356,30 +363,38 @@
             total = total + got[k * 24 : k * 24 + 24] * mask[k : k + 1]
         total = jnp.concatenate([total[0:8] + total[8:16], total[16:24]], 0)
         for g in range(group):
-            at = pl.ds(pl.multiple_of((i * group + g) * 16, 16), 16)
-            gbuf[at, :] = total[:, g * LANES : (g + 1) * LANES]
-        return c
-
-    lax.fori_loop(0, devices // group, gather_inverse, 0)
-
-    n = [pick(gbuf, r, 16) for r in range(8)]
-    n.append(pick(gbuf, 8, 16) + pick(gbuf, 9, 16))
-    full = [[n[0], n[1], n[2]], [n[1], n[3], n[4]], [n[2], n[4], n[5]]]
-    nu = [sum(full[k][l] * ju[l] for l in range(3)) for k in range(3)]
-    nv = [sum(full[k][l] * jv[l] for l in range(3)) for k in range(3)]
-    out = [
-        live - sum(ju[k] * nu[k] for k in range(3)),
-        -sum(ju[k] * nv[k] for k in range(3)),
-        live - sum(jv[k] * nv[k] for k in range(3)),
-        ru - sum(ju[k] * n[6 + k] for k in range(3)),
-        rv - sum(jv[k] * n[6 + k] for k in range(3)),
-        inv,
-        u,
-        v,
-    ]
-    for r in range(8):
-        tx2[pl.ds(r, devices, stride=8), :] = out[r]
-    send(1, tx2, rx2, 8)
+            gbuf[g * 16 : g * 16 + 16, :] = total[:, g * LANES : (g + 1) * LANES]
+        n = [gbuf[pl.ds(r, group, stride=16), :] for r in range(10)]
+        n[8] = n[8] + n[9]
+        old = [kept[r, pl.ds(pl.multiple_of(i * group, group), group), :] for r in range(12)]
+        ju, jv = old[0:3], old[3:6]
+        ru, rv, inv, u, v, live = old[6:12]
+        full = [[n[0], n[1], n[2]], [n[1], n[3], n[4]], [n[2], n[4], n[5]]]
+        nu = [sum(full[k][l] * ju[l] for l in range(3)) for k in range(3)]
+        nv = [sum(full[k][l] * jv[l] for l in range(3)) for k in range(3)]
+        out = [
+            live - sum(ju[k] * nu[k] for k in range(3)),
+            -sum(ju[k] * nv[k] for k in range(3)),
+            live - sum(jv[k] * nv[k] for k in range(3)),
+            ru - sum(ju[k] * n[6 + k] for k in range(3)),
+            rv - sum(jv[k] * n[6 + k] for k in range(3)),
+            inv,
+            u,
+            v,
+        ]
+        for r in range(8):
+            tx2[pl.ds(i * group * 8 + r, group, stride=8), :] = out[r]
+        for g in range(group):
+            peer = i * group + g
+
+            @pl.when(peer != me)
+            def _():
+                send_one(1, tx2, rx2, 8, peer)
+
+        return c
+
+    lax.fori_loop(0, devices // group, give_back, 0)
+    rx2[pl.ds(me * 8, 8)] = tx2[pl.ds(me * 8, 8)]
     wait(1, rx2, 8, recv_sem)
 
     muu, muv, mvv, eu, ev, inv, u, v = [pick(rx2, r, 8) for r in range(8)]
@@ -387,8 +402,8 @@
     cv = [-1.0 - v * v, u * v, u, None, inv, -v * inv]
 
     def combine(first, second):
-        kept = [a * b for a, b in (first, second) if b is not None]
-        return kept[0] if len(kept) == 1 else kept[0] + kept[1]
+        terms = [a * b for a, b in (first, second) if b is not None]
+        return terms[0] if len(terms) == 1 else terms[0] + terms[1]
 
     wu = [combine((muu, cu[a]), (muv, cv[a])) for a in range(6)]
     wv = [combine((muv, cu[a]), (mvv, cv[a])) for a in range(6)]
@@ -540,7 +555,8 @@
             vmem((levels * 24, LANES), F32),
             vmem((levels * 24, LANES), F32),
             vmem((levels * 24, LANES), F32),
-            vmem((devices * 16, LANES), F32),
+            vmem((math.gcd(devices, 8) * 16, LANES), F32),
+            vmem((12, devices, LANES), F32),
             vmem((devices * 32, LANES), F32),
             vmem((64, cams), F32),
             vmem((slots, cams), BF16),

time: 44.8 us -> 43.6 us (0.973)
  Pallas kernels: 42.5 us -> 41.4 us
    pallas_call x1, Pallas kernels: 42.5 us -> 41.4 us  [per_device(): pl.pallas_call(functools.partial(kernel, nx, ny), out_shape=jax.ShapeDtyp...]
where the time goes in v2:
time: 43.6 us; the launch traced here: 43.3 us
  Pallas kernels  41.4 us (95%)
  local copies, waits for them, and re-layouts  1.32 us (3%)
  between operations  0.64 us (1%)
    pallas_call x1, Pallas kernels, per_device(): pl.pallas_call(functools.partial(kernel, nx, ny), out_shape=jax.ShapeDtyp...  41.4 us
    squeeze x1, local copies, waits for them, and re-layouts, per_device(): return (out[0], out[1])  1.32 us

profile of v2, /device:TPU:0, one launch (start us, length us, event | category | flops | bytes accessed | tf_op | source)
XLA Modules:
  0.0 43.3 jit_solution(3615988088879427755)
XLA Ops:
  0.6 41.4 %shard_map.104 = f32[2,6,256]{2,1,0:T(8,128)} custom-call(f32[7,256]{1,0:T(8,128)} %cam_hbm.1, f32[3,4096]{1,0:T(4,128)} %pts_hbm.1, f32[2,1,32,128]{3,2,1,0:T(8,128)} %uv_hbm.1, s32[1,32,128]{2,1,0:T(8,128)} %oc_hbm.1, s32[1,32,128]{2,1,0:T(8,128)} %op_hbm.1, s32[1,32]{1,0:T(1,128)} %cnt_hbm.1, s32[1,16,32]{2,1,0:T(8,128)} %bitcast.5, s32[8,256]{1,0:T(8,128)} %es_hbm.1, ...), custom_call_target="tpu_custom_call" | custom-call | tf_op jit(solution)/shard_map/pallas_call | solution.py:537
  42.0 1.3 %slice_bitcast_fusion = (f32[6,256]{1,0:T(8,128)}, f32[6,256]{1,0:T(8,128)}) fusion(f32[2,6,256]{2,1,0:T(8,128)} %shard_map.104), kind=kLoop, calls=%fused_computation | loop fusion | bytes 24576 | tf_op jit(solution)/shard_map/squeeze | solution.py:570
